TPU v7x, 256 devices: a whole 4x4x8 slice. The times are simulated.
256 devices in a mesh: wide: 32 (over x_lo, z, core), rows: 8 (over y, x_hi).
Axes of the slice: x: 4 (x_hi: 2, x_lo: 2; x = x_hi * 2 + x_lo), y: 4, z: 8, core: 2. Of those that a mesh axis runs over, the one named last changes fastest.
Arguments:
- matrix: float32 [8192, 16384], P('rows', 'wide'), may hold values from -600 to 600, as said below
- pairing: int32 [2, 512], replicated, may hold values from 0 to 511, each once within a row
Outputs:
- rotated: float32 [8192, 16384], P('rows', 'wide')
Inputs may be any that keep to these rules, and one draw needn't show every extreme that they name: `matrix`: finite entries.
All inputs are finite; a program needn't handle non-finite values.
Results may differ from a plain program's by a relative error of at most 0.0001.
Values sent between devices are 32-bit elements; how exact they have to be, the bound alone decides.
A program may use at most 64 MiB of HBM per device.

v0:
```python
import jax
import jax.numpy as jnp
from jax import lax
from jax.sharding import PartitionSpec as P

NS_STEPS = 3


EPSILON = 1e-06
HIGH = lax.Precision.HIGHEST


def from_behind(value, axis, steps):
    count = lax.axis_size(axis)
    pairs = [(source, (source + steps) % count) for source in range(count)]
    return lax.ppermute(value, axis, pairs)


def generator(coupling, largest):
    half_cols = coupling.shape[0]
    identity = jnp.eye(half_cols, dtype=jnp.float32)
    top = jnp.concatenate([identity, coupling], axis=1)
    bottom = jnp.concatenate([-coupling.T, identity], axis=1)
    return jnp.concatenate([top, bottom], axis=0) * lax.rsqrt(1.0 + largest)


def shards(matrix, pairing):
    half_cols = matrix.shape[1] // 2
    current = matrix
    for round_index in range(pairing.shape[0]):
        columns = jnp.take(current, pairing[round_index], axis=1)
        partial_value = jnp.einsum(
            "ra,rb->ab", columns, columns, precision=HIGH, preferred_element_type=jnp.float32
        )
        gram = lax.psum(partial_value, "rows")
        norms = jnp.diagonal(gram)
        cross = gram[:half_cols, half_cols:]
        inverse = lax.rsqrt(norms + EPSILON)
        coupling = cross * inverse[:half_cols, None] * inverse[None, half_cols:]
        largest = lax.pmax(jnp.sum(coupling * coupling), "wide")
        rotation = generator(coupling, largest)
        for sweep in range(NS_STEPS):
            square = jnp.einsum(
                "ca,cb->ab", rotation, rotation, precision=HIGH, preferred_element_type=jnp.float32
            )
            rotation = 1.5 * rotation - 0.5 * jnp.dot(
                rotation, square, precision=HIGH, preferred_element_type=jnp.float32
            )
        product = jnp.dot(columns, rotation, precision=HIGH, preferred_element_type=jnp.float32)
        kept_block = product[:, :half_cols]
        moved_block = from_behind(product[:, half_cols:], "wide", 1)
        current = jnp.concatenate([kept_block, moved_block], axis=1)
    return current


def solution(mesh):
    in_specs = (P("rows", "wide"), P())
    out_specs = P("rows", "wide")
    return jax.shard_map(shards, mesh=mesh, in_specs=in_specs, out_specs=out_specs, check_vma=False)
```

profile of v0, /device:TPU:1, one launch (start us, length us, event | category | flops | bytes accessed | tf_op | source)
XLA Modules:
  0.0 416.0 jit_solution(11703738386899458625)
XLA Ops:
  6.5 0.8 fusion.55
  7.3 1.9 copy.12
  9.3 2.7 gather_fusion.2
  11.9 7.0 %fusion.6 = f32[512,512]{1,0:T(8,128)} fusion(f32[512,1024]{1,0:T(8,128)} %gather_fusion.2, pred[512]{0:T(512)(128)(4,1)S(1)} %compare_and_fusion.1), kind=kOutput, calls=%fused_computation.12 | convolution fusion | flops 3221749760 | bytes 3146240 | tf_op jit(solution)/shard_map/ra,rb->ab/dot_general | solution.py:32
  19.0 94.6 %all-reduce.3.cloned.1.call-done = f32[512,512]{1,0:T(8,128)} async-done(((f32[512,512]{1,0:T(8,128)}), f32[512,512]{1,0:T(8,128)}) %all-reduce.3.cloned.1.call-update) | async-done | bytes 1048592 | tf_op jit(solution)/shard_map/psum | solution.py:35
  113.7 8.4 %gather_fusion = f32[512]{0:T(512)S(1)} fusion(f32[512,512]{1,0:T(8,128)} %all-reduce.3.cloned.1.call-done, s32[512]{0:T(512)S(1)} %bitcast.37), kind=kCustom, calls=%fused_computation.2 | custom fusion | bytes 8192 | tf_op jit(solution)/shard_map/jit(diagonal)/cond/branch_0_fun/gather | solution.py:36
  122.1 1.8 multiply_reduce_fusion.1
  124.1 58.9 %pmax.14 = f32[]{:T(128)} all-reduce(f32[]{:T(128)} %get-tuple-element.8), channel_id=1, replica_groups=mesh['wide'=32,'rows'=8] {'wide'}, use_global_device_ids=true, to_apply=%region_2.4 | all-reduce | flops 1 | bytes 8 | tf_op jit(solution)/shard_map/pmax | solution.py:40
  183.6 1.9 fusion.33
  185.5 2.0 fusion.17
  187.6 1.9 fusion.58
  189.4 2.0 fusion.16
  191.4 1.9 fusion.59
  193.3 1.9 fusion.15
  195.2 4.0 fusion.4
  199.5 11.7 %collective-permute-done = f32[1024,256]{0,1:T(8,128)S(1)} collective-permute-done((f32[1024,256]{0,1:T(8,128)S(1)}, f32[1024,256]{0,1:T(8,128)S(1)}, u32[]{:S(2)}, u32[]{:S(2)}) %collective-permute-start) | collective-permute-done | bytes 1048608 | tf_op jit(solution)/shard_map/ppermute | solution.py:16
  211.2 0.2 pad_maximum_fusion
  211.5 2.7 gather_fusion.3
  214.1 7.0 %fusion.2 = f32[512,512]{0,1:T(8,128)} fusion(f32[512,1024]{1,0:T(8,128)} %gather_fusion.3, pred[512]{0:T(512)(128)(4,1)S(1)} %compare_and_fusion), kind=kOutput, calls=%fused_computation.8 | convolution fusion | flops 3221749760 | bytes 3146240 | tf_op jit(solution)/shard_map/ra,rb->ab/dot_general | solution.py:32
  221.2 88.2 %all-reduce.5.cloned.1.call-done = f32[512,512]{0,1:T(8,128)} async-done(((f32[512,512]{0,1:T(8,128)}), f32[512,512]{0,1:T(8,128)}) %all-reduce.5.cloned.1.call-update) | async-done | bytes 1048592 | tf_op jit(solution)/shard_map/psum | solution.py:35
  309.4 8.4 %gather_fusion.1 = f32[512]{0:T(512)S(1)} fusion(f32[512,512]{0,1:T(8,128)} %all-reduce.5.cloned.1.call-done, s32[512]{0:T(512)S(1)} %bitcast.38), kind=kCustom, calls=%fused_computation.3 | custom fusion | bytes 8192 | tf_op jit(solution)/shard_map/jit(diagonal)/cond/branch_0_fun/gather | solution.py:36
  317.8 1.8 multiply_reduce_fusion
  319.7 58.9 %pmax.15 = f32[]{:T(128)} all-reduce(f32[]{:T(128)} %get-tuple-element.6), channel_id=1, replica_groups=mesh['wide'=32,'rows'=8] {'wide'}, use_global_device_ids=true, to_apply=%region_5.7 | all-reduce | flops 1 | bytes 8 | tf_op jit(solution)/shard_map/pmax | solution.py:40
  379.3 1.9 fusion.30
  381.2 2.0 fusion.14
  383.2 1.9 fusion.60
  385.1 2.0 fusion.13
  387.0 1.9 fusion.61
  388.9 1.9 fusion.12
  390.8 4.1 fusion
  395.2 11.7 %collective-permute-done.1 = f32[1024,256]{0,1:T(8,128)S(1)} collective-permute-done((f32[1024,256]{0,1:T(8,128)S(1)}, f32[1024,256]{0,1:T(8,128)S(1)}, u32[]{:S(2)}, u32[]{:S(2)}) %collective-permute-start.1) | collective-permute-done | bytes 1048608 | tf_op jit(solution)/shard_map/ppermute | solution.py:16
  407.1 1.8 copy.20
  (29 shorter events, 1.1 us)
Async XLA Ops:
  6.5 107.1 %all-reduce.3.cloned.1.call-start = ((), (), s32[]{:S(2)}) async-start(), calls=%async_computation | async-start | bytes 2097152 | tf_op jit(solution)/shard_map/psum | solution.py:35
  18.9 290.4 %all-reduce.5.cloned.1.call-start = ((), (), s32[]{:S(2)}) async-start(), calls=%async_computation.1 | async-start | bytes 2097152 | tf_op jit(solution)/shard_map/psum | solution.py:35
  193.3 1.9 copy-start
  199.4 11.8 %collective-permute-start = (f32[1024,256]{0,1:T(8,128)S(1)}, f32[1024,256]{0,1:T(8,128)S(1)}, u32[]{:S(2)}, u32[]{:S(2)}) collective-permute-start(f32[1024,256]{0,1:T(8,128)S(1)} %get-tuple-element.13), channel_id=1, source_target_pairs={{0,8},{8,16},{16,24},{24,32},{32,40},{40,48},{48,56},{56,64},{64,7... | collective-permute-start | bytes 3145736 | tf_op jit(solution)/shard_map/ppermute | solution.py:16
  388.9 1.9 copy-start.1
  395.1 11.8 %collective-permute-start.1 = (f32[1024,256]{0,1:T(8,128)S(1)}, f32[1024,256]{0,1:T(8,128)S(1)}, u32[]{:S(2)}, u32[]{:S(2)}) collective-permute-start(f32[1024,256]{0,1:T(8,128)S(1)} %get-tuple-element.11), channel_id=1, source_target_pairs={{0,8},{8,16},{16,24},{24,32},{32,40},{40,48},{48,56},{56,64},{64,7... | collective-permute-start | bytes 3145736 | tf_op jit(solution)/shard_map/ppermute | solution.py:16
Sparse Core Ops, SparseCore 0:
  19.0 94.5 all-reduce.2
  221.3 87.9 all-reduce.4
where the time goes:
time: 424 us; the launch traced here: 416 us
  waiting for transfers between devices  206 us (49%)
  blocking collectives  118 us (28%)
  matrix products  45 us (11%)
  local copies, waits for them, and re-layouts  27.3 us (6%)
  between operations  15.4 us (4%)
    psum x2, waiting for transfers between devices, shards(): gram = lax.psum(partial_value, 'rows')  183 us
    pmax x2, blocking collectives, shards(): largest = lax.pmax(jnp.sum(coupling * coupling), 'wide')  118 us
    ppermute x2, waiting for transfers between devices, from_behind(): return lax.ppermute(value, axis, pairs)  23.4 us
    gather x2, local copies, waits for them, and re-layouts, shards(): norms = jnp.diagonal(gram)  16.8 us
    dot_general x2, matrix products, shards(): jnp.einsum('ra,rb->ab', columns, columns, precision=HIGH, preferred_eleme...  14 us
    dot_general x6, matrix products, shards(): jnp.dot(rotation, square, precision=HIGH, preferred_element_type=jnp.floa...  11.7 us
    dot_general x6, matrix products, shards(): jnp.einsum('ca,cb->ab', rotation, rotation, precision=HIGH, preferred_ele...  11.2 us
  transfers between devices with their start and end apart: 4, of which 4 were waited for; matrix products, arithmetic and copies ran while one was open for 0% of the time, Pallas kernels for 0%

commit v1 on v0

v1 whole, which is shorter than its diff:
```python
import functools

import jax
import jax.numpy as jnp
from jax import lax
from jax.experimental import pallas as pl
from jax.experimental.pallas import tpu as pltpu
from jax.sharding import PartitionSpec as P

EPSILON = 1e-06
F32 = jnp.float32
BF16 = jnp.bfloat16
CHUNKS = 4
MESH = pl.DeviceIdType.MESH


def split(value):
    high = value.astype(BF16)
    low = (value - high.astype(F32)).astype(BF16)
    return high, low


def dot(left, right, dims=((1,), (0,))):
    return lax.dot_general(left, right, (dims, ((), ())), preferred_element_type=F32)


def mul(left, right, dims=((1,), (0,))):
    return (
        dot(left[0], right[0], dims)
        + dot(left[0], right[1], dims)
        + dot(left[1], right[0], dims)
    )


def total(value):
    return jnp.sum(jnp.sum(value, axis=0, keepdims=True), axis=1, keepdims=True)


def kernel(
    n_wide, n_rows, n_rounds,
    x_ref, pairing_ref, out_ref,
    gram_out, gram_in, slice_out, slices, peak_out, peaks,
    current, cols_h, cols_l, u_h, u_l, v_h, v_l, moved,
    gram_acc, norm_acc,
    gram_send, gram_recv, slice_send, slice_recv, peak_send, peak_recv, move_send, move_recv,
):
    rows, width = x_ref.shape
    half = width // 2
    part = half // n_rows
    step = rows // CHUNKS
    me_w = lax.axis_index("wide")
    me_r = lax.axis_index("rows")

    barrier = pltpu.get_barrier_semaphore()
    for k in range(1, n_rows):
        pl.semaphore_signal(
            barrier, inc=1, device_id={"rows": lax.rem(me_r + k, n_rows)}, device_id_type=MESH
        )

    @pl.loop(1, n_wide)
    def _(k):
        pl.semaphore_signal(
            barrier, inc=1, device_id={"wide": lax.rem(me_w + k, n_wide)}, device_id_type=MESH
        )

    eye = (
        lax.broadcasted_iota(jnp.int32, (half, half), 0)
        == lax.broadcasted_iota(jnp.int32, (half, half), 1)
    ).astype(F32)

    for t in range(n_rounds):
        last = t == n_rounds - 1
        order = (
            lax.broadcasted_iota(jnp.int32, (width, width), 0) == pairing_ref[t : t + 1, :]
        ).astype(BF16)
        gram_acc[...] = jnp.zeros_like(gram_acc)
        norm_acc[...] = jnp.zeros_like(norm_acc)
        for chunk in range(CHUNKS):
            at = pl.ds(chunk * step, step)
            if t == 0:
                block = x_ref[at, :]
            else:
                pltpu.make_async_copy(
                    moved.at[t - 1, chunk], moved.at[t - 1, chunk], move_recv.at[t - 1, chunk]
                ).wait()
                block = jnp.concatenate([current[at, :], moved[t - 1, chunk]], axis=1)
            high, low = split(block)
            high = dot(high, order)
            low = dot(low, order)
            value = high + low
            norm_acc[...] += jnp.sum(value * value, axis=0, keepdims=True)
            high, low = high.astype(BF16), low.astype(BF16)
            cols_h[at, :] = high
            cols_l[at, :] = low
            gram_acc[...] += mul(
                (high[:, :half], low[:, :half]), (high[:, half:], low[:, half:]), ((0,), (0,))
            )

        for k in range(n_rows):
            gram_out[t, k, 0:part, :] = gram_acc[k * part : (k + 1) * part, :]
            gram_out[t, k, part : part + 1, :] = norm_acc[:, :half]
            gram_out[t, k, part + 1 : part + 2, :] = norm_acc[:, half:]
        if t == 0:
            pl.semaphore_wait(barrier, n_rows - 1 + n_wide - 1)
        for k in range(1, n_rows):
            peer = lax.rem(me_r + k, n_rows)
            pltpu.make_async_remote_copy(
                src_ref=gram_out.at[t, peer],
                dst_ref=gram_in.at[t, me_r],
                send_sem=gram_send.at[t],
                recv_sem=gram_recv.at[t],
                device_id={"rows": peer},
                device_id_type=MESH,
            ).start()
        gram_in[t, me_r] = gram_out[t, me_r]
        seven = pl.ds(0, n_rows - 1)
        pltpu.make_async_copy(gram_in.at[t, seven], gram_in.at[t, seven], gram_recv.at[t]).wait()
        summed = gram_in[t, 0]
        for k in range(1, n_rows):
            summed = summed + gram_in[t, k]
        inverse_a = lax.rsqrt(summed[part : part + 1, :] + EPSILON)
        inverse_b = lax.rsqrt(summed[part + 1 : part + 2, :] + EPSILON)
        mine = (
            lax.broadcasted_iota(jnp.int32, (part, half), 0) + me_r * part
            == lax.broadcasted_iota(jnp.int32, (part, half), 1)
        )
        column = jnp.sum(jnp.where(mine, inverse_a, 0.0), axis=1, keepdims=True)
        share = summed[0:part, :] * column * inverse_b
        slice_out[t] = share
        slices[t, me_r] = share
        for k in range(1, n_rows):
            peer = lax.rem(me_r + k, n_rows)
            pltpu.make_async_remote_copy(
                src_ref=slice_out.at[t],
                dst_ref=slices.at[t, me_r],
                send_sem=slice_send.at[t],
                recv_sem=slice_recv.at[t],
                device_id={"rows": peer},
                device_id_type=MESH,
            ).start()
        pltpu.make_async_copy(slices.at[t, seven], slices.at[t, seven], slice_recv.at[t]).wait()
        coupling = slices[t].reshape(half, half)
        own = total(coupling * coupling)
        peak_out[t] = jnp.broadcast_to(own, peak_out.shape[1:])
        peaks[t, me_w] = jnp.broadcast_to(own, peak_out.shape[1:])

        @pl.loop(1, n_wide)
        def _(k):
            pltpu.make_async_remote_copy(
                src_ref=peak_out.at[t],
                dst_ref=peaks.at[t, me_w],
                send_sem=peak_send.at[t],
                recv_sem=peak_recv.at[t],
                device_id={"wide": lax.rem(me_w + k, n_wide)},
                device_id_type=MESH,
            ).start()

        flipped = coupling.T
        c = split(coupling)
        ct = split(flipped)
        for chunk in range(CHUNKS):
            at = pl.ds(chunk * step, step)
            high, low = cols_h[at, :], cols_l[at, :]
            a = (high[:, :half], low[:, :half])
            b = (high[:, half:], low[:, half:])
            u = a[0].astype(F32) + a[1].astype(F32) - mul(b, ct)
            v = b[0].astype(F32) + b[1].astype(F32) + mul(a, c)
            u_h[at, :], u_l[at, :] = split(u)
            v_h[at, :], v_l[at, :] = split(v)
        scale = 1.0 / (1.0 + own)
        powers = []
        for left, right in ((c, ct), (ct, c)):
            first = (eye + mul(left, right)) * scale
            pieces = split(first)
            second = mul(pieces, pieces)
            third = mul(split(second), pieces)
            powers.append((first, second, third))

        others = pl.ds(0, n_wide - 1)
        pltpu.make_async_copy(peaks.at[t, others], peaks.at[t, others], peak_recv.at[t]).wait()
        largest = jnp.max(peaks[t], axis=0)[0:1, 0:1]
        root = lax.rsqrt(1.0 + largest)
        ratio = (1.0 + own) / (1.0 + largest)
        factors = []
        for first, second, third in powers:
            n1 = (2.25 * ratio) * first - (1.5 * ratio * ratio) * second
            n1 = n1 + (0.25 * ratio * ratio * ratio) * third
            t1 = split(1.5 * eye - 0.5 * n1)
            q1 = root * (1.5 * eye - (0.5 * ratio) * first)
            n2 = mul(split(mul(split(n1), t1)), t1)
            q2 = mul(split(q1), t1)
            t2 = split(1.5 * eye - 0.5 * n2)
            factors.append(split(mul(split(q2), t2)))

        for chunk in range(CHUNKS):
            at = pl.ds(chunk * step, step)
            moved[n_rounds + t, chunk] = mul((v_h[at, :], v_l[at, :]), factors[1])
            pltpu.make_async_remote_copy(
                src_ref=moved.at[n_rounds + t, chunk],
                dst_ref=moved.at[t, chunk],
                send_sem=move_send.at[t, chunk],
                recv_sem=move_recv.at[t, chunk],
                device_id={"wide": lax.rem(me_w + 1, n_wide)},
                device_id_type=MESH,
            ).start()
        for chunk in range(CHUNKS):
            at = pl.ds(chunk * step, step)
            kept = mul((u_h[at, :], u_l[at, :]), factors[0])
            if last:
                out_ref[at, 0:half] = kept
            else:
                current[at, :] = kept
        pltpu.make_async_copy(gram_out.at[t, seven], gram_out.at[t, seven], gram_send.at[t]).wait()
        pltpu.make_async_copy(slices.at[t, seven], slices.at[t, seven], slice_send.at[t]).wait()
        pltpu.make_async_copy(peaks.at[t, others], peaks.at[t, others], peak_send.at[t]).wait()
        if last:
            for chunk in range(CHUNKS):
                at = pl.ds(chunk * step, step)
                pltpu.make_async_copy(
                    moved.at[t, chunk], moved.at[t, chunk], move_recv.at[t, chunk]
                ).wait()
                out_ref[at, half:width] = moved[t, chunk]
    for t in range(n_rounds):
        for chunk in range(CHUNKS):
            sent = moved.at[n_rounds + t, chunk]
            pltpu.make_async_copy(sent, sent, move_send.at[t, chunk]).wait()


def solution(mesh):
    n_wide, n_rows = mesh.shape["wide"], mesh.shape["rows"]

    def shards(matrix, pairing):
        rows, width = matrix.shape
        half = width // 2
        part = half // n_rows
        n_rounds = pairing.shape[0]
        step = rows // CHUNKS
        vmem = pl.BlockSpec(memory_space=pltpu.VMEM)
        dma = pltpu.SemaphoreType.DMA
        return pl.pallas_call(
            functools.partial(kernel, n_wide, n_rows, n_rounds),
            out_shape=jax.ShapeDtypeStruct(matrix.shape, F32),
            in_specs=[vmem, vmem],
            out_specs=vmem,
            scratch_shapes=[
                pltpu.VMEM((n_rounds, n_rows, part + 8, half), F32),
                pltpu.VMEM((n_rounds, n_rows, part + 8, half), F32),
                pltpu.VMEM((n_rounds, part, half), F32),
                pltpu.VMEM((n_rounds, n_rows, part, half), F32),
                pltpu.VMEM((n_rounds, 8, 128), F32),
                pltpu.VMEM((n_rounds, n_wide, 8, 128), F32),
                pltpu.VMEM((rows, half), F32),
                pltpu.VMEM((rows, width), BF16),
                pltpu.VMEM((rows, width), BF16),
                pltpu.VMEM((rows, half), BF16),
                pltpu.VMEM((rows, half), BF16),
                pltpu.VMEM((rows, half), BF16),
                pltpu.VMEM((rows, half), BF16),
                pltpu.VMEM((2 * n_rounds, CHUNKS, step, half), F32),
                pltpu.VMEM((half, half), F32),
                pltpu.VMEM((1, width), F32),
                dma((n_rounds,)), dma((n_rounds,)), dma((n_rounds,)), dma((n_rounds,)),
                dma((n_rounds,)), dma((n_rounds,)), dma((n_rounds, CHUNKS)), dma((n_rounds, CHUNKS)),
            ],
            compiler_params=pltpu.CompilerParams(
                collective_id=0, has_side_effects=True, vmem_limit_bytes=48 * 1024 * 1024
            ),
        )(matrix, pairing)

    return jax.shard_map(
        shards, mesh=mesh, in_specs=(P("rows", "wide"), P()), out_specs=P("rows", "wide"),
        check_vma=False,
    )
```

time: 424 us -> 82.1 us (0.19)
  the two profiles are of different devices: /device:TPU:1 before, /device:TPU:4 now
where the time goes in v1:
time: 82.1 us; the launch traced here: 81.9 us
  Pallas kernels  78.3 us (95%)
  local copies, waits for them, and re-layouts  3.6 us (4%)
    pallas_call x1, Pallas kernels, shards(): pl.pallas_call(functools.partial(kernel, n_wide, n_rows, n_rounds), out_s...  78.3 us
    unnamed x5, local copies, waits for them, and re-layouts  3.6 us

profile of v1, /device:TPU:4, one launch (start us, length us, event | category | flops | bytes accessed | tf_op | source)
XLA Modules:
  0.0 81.9 jit_solution(7720597912659222827)
XLA Ops:
  0.0 0.0 copy-start
  0.0 1.6 %copy-done = f32[1024,512]{1,0:T(8,128)S(1)} copy-done((f32[1024,512]{1,0:T(8,128)S(1)}, f32[1024,512]{1,0:T(8,128)}, u32[]{:S(2)}) %copy-start) | copy-done | bytes 2097176
  1.6 0.0 copy-start.1
  1.6 0.7 copy-done.1
  2.3 78.3 %shard_map.28 = f32[1024,512]{1,0:T(8,128)S(1)} custom-call(f32[1024,512]{1,0:T(8,128)S(1)} %copy-done, s32[2,512]{1,0:T(2,128)S(1)} %copy-done.1), custom_call_target="tpu_custom_call" | custom-call | tf_op jit(solution)/shard_map/pallas_call | solution.py:240
  80.6 1.3 %copy.4 = f32[1024,512]{1,0:T(8,128)} copy(f32[1024,512]{1,0:T(8,128)S(1)} %shard_map.28) | data formatting | bytes 4194304
Async XLA Ops:
  0.0 1.6 %copy-start = (f32[1024,512]{1,0:T(8,128)S(1)}, f32[1024,512]{1,0:T(8,128)}, u32[]{:S(2)}) copy-start(f32[1024,512]{1,0:T(8,128)} %x_ref.1) | copy-start | bytes 6291460
  1.6 0.7 copy-start.1

commit v2 on v1

v2 whole, which is shorter than its diff:
```python
import functools

import jax
import jax.numpy as jnp
from jax import lax
from jax.experimental import pallas as pl
from jax.experimental.pallas import tpu as pltpu
from jax.sharding import PartitionSpec as P

EPSILON = 1e-06
F32 = jnp.float32
BF16 = jnp.bfloat16
CHUNKS = 4
RAW = ((0, 256), (256, 192))
PIECES = ((448, 128), (576, 192), (768, 256))
EARLY = 2
RELAY = ((0, 256), (256, 192))
MESH = pl.DeviceIdType.MESH


def split(value):
    high = value.astype(BF16)
    low = (value - high.astype(F32)).astype(BF16)
    return high, low


def dot(left, right, dims=((1,), (0,))):
    return lax.dot_general(left, right, (dims, ((), ())), preferred_element_type=F32)


def mul(left, right, dims=((1,), (0,))):
    return (
        dot(left[0], right[0], dims)
        + dot(left[0], right[1], dims)
        + dot(left[1], right[0], dims)
    )


def total(value):
    return jnp.sum(jnp.sum(value, axis=0, keepdims=True), axis=1, keepdims=True)


def ring(distance, size):
    return min(distance, size - distance)


def row_peers(me_r, n_rows):
    n_y = n_rows // 2
    y, x = me_r // 2, me_r % 2
    offsets = [(dy, dx) for dy in range(n_y) for dx in range(2) if dy or dx]
    offsets.sort(key=lambda o: -(ring(o[0], n_y) + 2 * o[1]))
    return [((y + dy) % n_y) * 2 + (x + dx) % 2 for dy, dx in offsets]


def column_peers(me_w, n_wide):
    n_z = n_wide // 4
    x, z, core = me_w // (2 * n_z), (me_w // 2) % n_z, me_w % 2
    offsets = [(dz, dc) for dz in range(n_z) for dc in range(2) if dz or dc]
    offsets.sort(key=lambda o: -(ring(o[0], n_z) + 0.1 * o[1]))
    return [x * (2 * n_z) + ((z + dz) % n_z) * 2 + (core + dc) % 2 for dz, dc in offsets]


def wait(ref, sem):
    pltpu.make_async_copy(ref, ref, sem).wait()


def kernel(
    n_wide, n_rows, n_rounds,
    x_hbm, pairing_hbm, out_ref,
    x_ref, pairing_ref,
    gram_out, gram_in, part_out, parts, slice_out, slices, peak_out, peaks,
    raw_out, raw_in, v_out, v_in, behinds, crosses, cross, pass_in,
    cols_h, cols_l, u_h, u_l, v_h, v_l, gram_acc, norm_acc,
    x_sem, pairing_sem,
    gram_send, gram_recv, part_send, part_recv, slice_send, slice_recv, peak_send, peak_recv,
    raw_send, raw_recv, v_send, v_recv, relay_send, relay_recv, pass_send, pass_recv,
    c_send, c_recv, d_send, d_recv,
):
    rows, width = x_ref.shape
    half = width // 2
    part = half // n_rows
    step = rows // CHUNKS
    me_w = lax.axis_index("wide")
    me_r = lax.axis_index("rows")
    following = {"wide": lax.rem(me_w + 1, n_wide)}
    column = n_wide // 2
    first_z = lax.rem(me_w, column) == 0
    last_z = lax.rem(me_w, column) == column - 1
    next_z = {"wide": (me_w // column) * column + lax.rem(me_w + 1, column)}
    partner = {"wide": lax.rem(me_w + column, n_wide)}
    me_x, me_c = me_w // column, lax.rem(me_w, column)
    along_rows = [{"rows": peer} for peer in row_peers(me_r, n_rows)]
    along_column = [{"wide": peer} for peer in column_peers(me_w, n_wide)]

    def rows_of(pair):
        far = [{"wide": pair, "rows": device["rows"]} for device in along_rows]
        return far + [{"wide": pair, "rows": me_r}]


    def send(source, target, send_sem, recv_sem, device):
        pltpu.make_async_remote_copy(
            src_ref=source, dst_ref=target, send_sem=send_sem, recv_sem=recv_sem,
            device_id=device, device_id_type=MESH,
        ).start()

    pltpu.make_async_copy(pairing_hbm, pairing_ref, pairing_sem).start()
    for chunk in range(CHUNKS):
        at = pl.ds(chunk * step, step)
        pltpu.make_async_copy(x_hbm.at[at], x_ref.at[at], x_sem.at[chunk]).start()
    barrier = pltpu.get_barrier_semaphore()

    def greet(devices):
        for device in devices:
            pl.semaphore_signal(barrier, inc=1, device_id=device, device_id_type=MESH)

    known = along_rows + along_column + rows_of(partner["wide"])
    greet(known)

    @pl.when(last_z)
    def _():
        greet([following])

    @pl.when(first_z)
    def _():
        greet([{"wide": lax.rem(me_w + n_wide - 1, n_wide)}])


    eye = (
        lax.broadcasted_iota(jnp.int32, (half, half), 0)
        == lax.broadcasted_iota(jnp.int32, (half, half), 1)
    ).astype(F32)
    mine = (
        lax.broadcasted_iota(jnp.int32, (part, half), 0) + me_r * part
        == lax.broadcasted_iota(jnp.int32, (part, half), 1)
    )
    pltpu.make_async_copy(pairing_hbm, pairing_ref, pairing_sem).wait()
    factors = None
    raw_rows = sum(size for _, size in RAW)

    def send_raw(t, k):
        at = pl.ds(*RAW[k])
        send(raw_out.at[t, at], raw_in.at[t, at], raw_send.at[t, k], raw_recv.at[t, k], next_z)

    def finished(t, chunk):
        at = pl.ds(chunk * step, step)
        kept = mul((u_h[at, :], u_l[at, :]), factors[0])
        for k, (start, size) in enumerate(PIECES):
            if chunk * step <= start < (chunk + 1) * step:
                rows_at = pl.ds(start, size)
                wait(v_in.at[t, rows_at], v_recv.at[t, k])
                v_h[rows_at, :], v_l[rows_at, :] = split(v_in[t, rows_at, :])
        for k, (start, size) in enumerate(RELAY):
            if chunk * step <= start < (chunk + 1) * step:
                rows_at = pl.ds(start, size)

                @pl.when(first_z)
                def _():
                    wait(v_in.at[t, rows_at], relay_recv.at[t, k])
                    v_h[rows_at, :], v_l[rows_at, :] = split(v_in[t, rows_at, :])

        return jnp.concatenate([kept, mul((v_h[at, :], v_l[at, :]), factors[1])], axis=1)

    for t in range(n_rounds):
        order = (
            lax.broadcasted_iota(jnp.int32, (width, width), 0) == pairing_ref[t : t + 1, :]
        ).astype(BF16)
        gram_acc[...] = jnp.zeros_like(gram_acc)
        norm_acc[...] = jnp.zeros_like(norm_acc)
        for chunk in range(CHUNKS):
            at = pl.ds(chunk * step, step)
            if t == 0:
                pltpu.make_async_copy(x_hbm.at[at], x_ref.at[at], x_sem.at[chunk]).wait()
                block = x_ref[at, :]
            else:
                block = finished(t - 1, chunk)
            high, low = split(block)
            high = dot(high, order)
            low = dot(low, order)
            value = high + low
            if chunk * step < raw_rows:
                size = min(step, raw_rows - chunk * step)
                raw_out[t, pl.ds(chunk * step, size), :] = value[:size]
                if t > 0:
                    for k, (start, _) in enumerate(RAW):
                        if chunk * step <= start < (chunk + 1) * step:
                            send_raw(t, k)
            norm_acc[...] += jnp.sum(value * value, axis=0, keepdims=True)
            high, low = high.astype(BF16), low.astype(BF16)
            cols_h[at, :] = high
            cols_l[at, :] = low
            gram_acc[...] += mul(
                (high[:, :half], low[:, :half]), (high[:, half:], low[:, half:]), ((0,), (0,))
            )

        for k in range(n_rows):
            gram_out[t, k, 0:part, :] = gram_acc[k * part : (k + 1) * part, :]
            gram_out[t, k, part : part + 1, :] = norm_acc[:, :half]
            gram_out[t, k, part + 1 : part + 2, :] = norm_acc[:, half:]
        if t == 0:
            crossing = jnp.where(jnp.logical_or(first_z, last_z), 1, 0)
            pl.semaphore_wait(barrier, len(known) + crossing)
        for device in along_rows:
            send(
                gram_out.at[t, device["rows"]], gram_in.at[t, me_r],
                gram_send.at[t], gram_recv.at[t], device,
            )
        if t == 0:
            for k in range(len(RAW)):
                send_raw(t, k)
        gram_in[t, me_r] = gram_out[t, me_r]
        seven = pl.ds(0, n_rows - 1)
        all_but_one = pl.ds(0, 2 * n_rows - 1)
        wait(gram_in.at[t, seven], gram_recv.at[t])
        summed = gram_in[t, 0]
        for k in range(1, n_rows):
            summed = summed + gram_in[t, k]
        inverse_a = lax.rsqrt(summed[part : part + 1, :] + EPSILON)
        inverse_b = lax.rsqrt(summed[part + 1 : part + 2, :] + EPSILON)
        scaled = jnp.sum(jnp.where(mine, inverse_a, 0.0), axis=1, keepdims=True)
        share = summed[0:part, :] * scaled * inverse_b

        square = jnp.broadcast_to(total(share * share), (8, 128))
        part_out[t] = square
        place = me_x * n_rows + me_r
        parts[t, place] = square
        across = rows_of(partner["wide"])
        for device in across[:-1] + along_rows + across[-1:]:
            send(part_out.at[t], parts.at[t, place], part_send.at[t], part_recv.at[t], device)
        slice_out[t] = share
        slices[t, me_r] = share
        for device in along_rows:
            send(slice_out.at[t], slices.at[t, me_r], slice_send.at[t], slice_recv.at[t], device)
        wait(parts.at[t, all_but_one], part_recv.at[t])
        peak = parts[t, me_x * n_rows]
        other = parts[t, (1 - me_x) * n_rows]
        for k in range(1, n_rows):
            peak = peak + parts[t, me_x * n_rows + k]
            other = other + parts[t, (1 - me_x) * n_rows + k]
        own = peak[0:1, 0:1]
        peak = jnp.maximum(peak, other)
        peak_out[t] = peak
        peaks[t, me_c] = peak
        for device in along_column:
            send(peak_out.at[t], peaks.at[t, me_c], peak_send.at[t], peak_recv.at[t], device)

        wait(slices.at[t, seven], slice_recv.at[t])
        send(slices.at[t], behinds.at[t], c_send.at[t], c_recv.at[t], following)

        @pl.when(last_z)
        def _():
            send(slices.at[t], crosses.at[t], d_send.at[t], d_recv.at[t], next_z)

        coupling = slices[t].reshape(half, half)
        c = split(coupling)
        for k, (start, size) in enumerate(PIECES):
            at = pl.ds(start, size)
            high, low = cols_h[at, :], cols_l[at, :]
            v = high[:, half:].astype(F32) + low[:, half:].astype(F32)
            v_out[t, at, :] = v + mul((high[:, :half], low[:, :half]), c)

            @pl.when(last_z)
            def _():
                send(v_out.at[t, at], pass_in.at[t, at], pass_send.at[t, k], pass_recv.at[t, k], partner)


        wait(behinds.at[t], c_recv.at[t])
        behind = behinds[t].reshape(half, half)

        @pl.when(first_z)
        def _():
            wait(crosses.at[t], d_recv.at[t])
            cross[...] = crosses[t].reshape(half, half)

        @pl.when(jnp.logical_not(first_z))
        def _():
            cross[...] = behind

        c_cross = split(cross[...])
        for k, (start, size) in enumerate(RAW):
            at = pl.ds(start, size)
            wait(raw_in.at[t, at], raw_recv.at[t, k])
            left, right = raw_in[t, at, 0:half], raw_in[t, at, half:width]
            v = right + mul(split(left), c_cross)
            v_out[t, at, :] = v
            v_h[at, :], v_l[at, :] = split(v)

        ct = split(coupling.T)
        for chunk in range(CHUNKS):
            at = pl.ds(chunk * step, step)
            high, low = cols_h[at, :], cols_l[at, :]
            u = high[:, :half].astype(F32) + low[:, :half].astype(F32)
            u_h[at, :], u_l[at, :] = split(u - mul((high[:, half:], low[:, half:]), ct))

        def powers(left, right, bound):
            first = (eye + mul(left, right)) * (1.0 / (1.0 + bound))
            pieces = split(first)
            second = mul(pieces, pieces)
            return first, second, mul(split(second), pieces)

        kept_powers = powers(c, ct, own)
        c = split(behind)
        ct = split(behind.T)
        own_behind = total(behind * behind)
        moved_powers = powers(ct, c, own_behind)

        others = pl.ds(0, column - 1)
        wait(peaks.at[t, others], peak_recv.at[t])

        @pl.when(first_z)
        def _():
            for k, (start, size) in enumerate(RELAY):
                at = pl.ds(start, size)
                send(v_out.at[t, at], v_in.at[t, at], relay_send.at[t, k], relay_recv.at[t, k], partner)

        @pl.when(jnp.logical_not(last_z))
        def _():
            for k, (start, size) in enumerate(PIECES):
                at = pl.ds(start, size)
                send(v_out.at[t, at], v_in.at[t, at], v_send.at[t, k], v_recv.at[t, k], following)

        def forward(k):
            at = pl.ds(*PIECES[k])
            wait(pass_in.at[t, at], pass_recv.at[t, k])
            send(pass_in.at[t, at], v_in.at[t, at], v_send.at[t, k], v_recv.at[t, k], next_z)

        @pl.when(last_z)
        def _():
            for k in range(EARLY):
                forward(k)

        largest = jnp.max(peaks[t], axis=0)[0:1, 0:1]
        root = lax.rsqrt(1.0 + largest)
        factors = []
        for (first, second, third), bound in ((kept_powers, own), (moved_powers, own_behind)):
            ratio = (1.0 + bound) / (1.0 + largest)
            n1 = (2.25 * ratio) * first - (1.5 * ratio * ratio) * second
            n1 = n1 + (0.25 * ratio * ratio * ratio) * third
            t1 = split(1.5 * eye - 0.5 * n1)
            q1 = root * (1.5 * eye - (0.5 * ratio) * first)
            n2 = mul(split(mul(split(n1), t1)), t1)
            q2 = mul(split(q1), t1)
            t2 = split(1.5 * eye - 0.5 * n2)
            factors.append(split(mul(split(q2), t2)))

        @pl.when(last_z)
        def _():
            for k in range(EARLY, len(PIECES)):
                forward(k)

    for chunk in range(CHUNKS):
        at = pl.ds(chunk * step, step)
        out_ref[at, :] = finished(n_rounds - 1, chunk)

    for t in range(n_rounds):
        wait(gram_out.at[t, seven], gram_send.at[t])
        wait(parts.at[t, all_but_one], part_send.at[t])
        wait(slices.at[t, seven], slice_send.at[t])
        wait(peaks.at[t, others], peak_send.at[t])
        wait(behinds.at[t], c_send.at[t])
        for k, (start, size) in enumerate(RAW):
            wait(raw_out.at[t, pl.ds(start, size)], raw_send.at[t, k])
        for k, (start, size) in enumerate(PIECES):
            wait(v_out.at[t, pl.ds(start, size)], v_send.at[t, k])

        @pl.when(last_z)
        def _():
            wait(crosses.at[t], d_send.at[t])
            for k, (start, size) in enumerate(PIECES):
                wait(v_out.at[t, pl.ds(start, size)], pass_send.at[t, k])

        @pl.when(first_z)
        def _():
            for k, (start, size) in enumerate(RELAY):
                wait(v_out.at[t, pl.ds(start, size)], relay_send.at[t, k])


def solution(mesh):
    n_wide, n_rows = mesh.shape["wide"], mesh.shape["rows"]

    def shards(matrix, pairing):
        rows, width = matrix.shape
        half = width // 2
        part = half // n_rows
        n_rounds = pairing.shape[0]
        raw_rows = sum(size for _, size in RAW)
        hbm = pl.BlockSpec(memory_space=pltpu.HBM)
        dma = pltpu.SemaphoreType.DMA

        def f32(*shape):
            return pltpu.VMEM(shape, F32)

        def bf16(*shape):
            return pltpu.VMEM(shape, BF16)

        return pl.pallas_call(
            functools.partial(kernel, n_wide, n_rows, n_rounds),
            out_shape=jax.ShapeDtypeStruct(matrix.shape, F32),
            in_specs=[hbm, hbm],
            out_specs=pl.BlockSpec(memory_space=pltpu.VMEM),
            scratch_shapes=[
                f32(rows, width),
                pltpu.VMEM(pairing.shape, pairing.dtype),
                f32(n_rounds, n_rows, part + 8, half),
                f32(n_rounds, n_rows, part + 8, half),
                f32(n_rounds, 8, 128),
                f32(n_rounds, 2 * n_rows, 8, 128),
                f32(n_rounds, part, half),
                f32(n_rounds, n_rows, part, half),
                f32(n_rounds, 8, 128),
                f32(n_rounds, n_wide // 2, 8, 128),
                f32(n_rounds, raw_rows, width),
                f32(n_rounds, raw_rows, width),
                f32(n_rounds, rows, half),
                f32(n_rounds, rows, half),
                f32(n_rounds, n_rows, part, half),
                f32(n_rounds, n_rows, part, half),
                f32(half, half),
                f32(n_rounds, rows, half),
                bf16(rows, width), bf16(rows, width),
                bf16(rows, half), bf16(rows, half), bf16(rows, half), bf16(rows, half),
                f32(half, half),
                f32(1, width),
                dma((CHUNKS,)), dma,
                dma((n_rounds,)), dma((n_rounds,)), dma((n_rounds,)), dma((n_rounds,)),
                dma((n_rounds,)), dma((n_rounds,)), dma((n_rounds,)), dma((n_rounds,)),
                dma((n_rounds, len(RAW))), dma((n_rounds, len(RAW))),
                dma((n_rounds, len(PIECES))), dma((n_rounds, len(PIECES))),
                dma((n_rounds, len(RELAY))), dma((n_rounds, len(RELAY))),
                dma((n_rounds, len(PIECES))), dma((n_rounds, len(PIECES))),
                dma((n_rounds,)), dma((n_rounds,)), dma((n_rounds,)), dma((n_rounds,)),
            ],
            compiler_params=pltpu.CompilerParams(
                collective_id=0, has_side_effects=True, vmem_limit_bytes=48 * 1024 * 1024
            ),
        )(matrix, pairing)

    return jax.shard_map(
        shards, mesh=mesh, in_specs=(P("rows", "wide"), P()), out_specs=P("rows", "wide"),
        check_vma=False,
    )
```

time: 82.1 us -> 73.9 us (0.900)
  the two profiles are of different devices: /device:TPU:4 before, /device:TPU:1 now
where the time goes in v2:
time: 73.9 us; the launch traced here: 73.8 us
  Pallas kernels  70.2 us (95%)
  local copies, waits for them, and re-layouts  3.6 us (5%)
    pallas_call x1, Pallas kernels, shards(): pl.pallas_call(functools.partial(kernel, n_wide, n_rows, n_rounds), out_s...  70.2 us
    unnamed x5, local copies, waits for them, and re-layouts  3.6 us

profile of v2, /device:TPU:1, one launch (start us, length us, event | category | flops | bytes accessed | tf_op | source)
XLA Modules:
  0.0 73.8 jit_solution(3409281912594656967)
XLA Ops:
  0.0 0.0 copy-start
  0.0 1.6 %copy-done = f32[1024,512]{1,0:T(8,128)S(1)} copy-done((f32[1024,512]{1,0:T(8,128)S(1)}, f32[1024,512]{1,0:T(8,128)}, u32[]{:S(2)}) %copy-start) | copy-done | bytes 2097176
  1.6 0.0 copy-start.1
  1.6 0.7 copy-done.1
  2.3 70.2 %shard_map.28 = f32[1024,512]{1,0:T(8,128)S(1)} custom-call(f32[1024,512]{1,0:T(8,128)S(1)} %copy-done, s32[2,512]{1,0:T(2,128)S(1)} %copy-done.1), custom_call_target="tpu_custom_call" | custom-call | tf_op jit(solution)/shard_map/pallas_call | solution.py:395
  72.5 1.3 %copy.4 = f32[1024,512]{1,0:T(8,128)} copy(f32[1024,512]{1,0:T(8,128)S(1)} %shard_map.28) | data formatting | bytes 4194304
Async XLA Ops:
  0.0 1.6 %copy-start = (f32[1024,512]{1,0:T(8,128)S(1)}, f32[1024,512]{1,0:T(8,128)}, u32[]{:S(2)}) copy-start(f32[1024,512]{1,0:T(8,128)} %x_hbm.1) | copy-start | bytes 6291460
  1.6 0.7 copy-start.1

commit v3 on v2

--- a/solution.py
+++ b/solution.py
@@ -284,6 +284,12 @@
             v_out[t, at, :] = v
             v_h[at, :], v_l[at, :] = split(v)
 
+        @pl.when(first_z)
+        def _():
+            for k, (start, size) in enumerate(RELAY):
+                at = pl.ds(start, size)
+                send(v_out.at[t, at], v_in.at[t, at], relay_send.at[t, k], relay_recv.at[t, k], partner)
+
         ct = split(coupling.T)
         for chunk in range(CHUNKS):
             at = pl.ds(chunk * step, step)
@@ -305,12 +311,6 @@
 
         others = pl.ds(0, column - 1)
         wait(peaks.at[t, others], peak_recv.at[t])
-
-        @pl.when(first_z)
-        def _():
-            for k, (start, size) in enumerate(RELAY):
-                at = pl.ds(start, size)
-                send(v_out.at[t, at], v_in.at[t, at], relay_send.at[t, k], relay_recv.at[t, k], partner)
 
         @pl.when(jnp.logical_not(last_z))
         def _():

time: 73.9 us -> 69.7 us (0.943)
  Pallas kernels: 70.2 us -> 66 us
    pallas_call x1, Pallas kernels: 70.2 us -> 66 us  [shards(): pl.pallas_call(functools.partial(kernel, n_wide, n_rows, n_rounds), out_s...]
where the time goes in v3:
time: 69.7 us; the launch traced here: 69.6 us
  Pallas kernels  66 us (95%)
  local copies, waits for them, and re-layouts  3.6 us (5%)
    pallas_call x1, Pallas kernels, shards(): pl.pallas_call(functools.partial(kernel, n_wide, n_rows, n_rounds), out_s...  66 us
    unnamed x5, local copies, waits for them, and re-layouts  3.6 us

profile of v3, /device:TPU:1, one launch (start us, length us, event | category | flops | bytes accessed | tf_op | source)
XLA Modules:
  0.0 69.6 jit_solution(14529295398333303398)
XLA Ops:
  0.0 0.0 copy-start
  0.0 1.6 %copy-done = f32[1024,512]{1,0:T(8,128)S(1)} copy-done((f32[1024,512]{1,0:T(8,128)S(1)}, f32[1024,512]{1,0:T(8,128)}, u32[]{:S(2)}) %copy-start) | copy-done | bytes 2097176
  1.6 0.0 copy-start.1
  1.6 0.7 copy-done.1
  2.3 66.0 %shard_map.28 = f32[1024,512]{1,0:T(8,128)S(1)} custom-call(f32[1024,512]{1,0:T(8,128)S(1)} %copy-done, s32[2,512]{1,0:T(2,128)S(1)} %copy-done.1), custom_call_target="tpu_custom_call" | custom-call | tf_op jit(solution)/shard_map/pallas_call | solution.py:395
  68.3 1.3 %copy.4 = f32[1024,512]{1,0:T(8,128)} copy(f32[1024,512]{1,0:T(8,128)S(1)} %shard_map.28) | data formatting | bytes 4194304
Async XLA Ops:
  0.0 1.6 %copy-start = (f32[1024,512]{1,0:T(8,128)S(1)}, f32[1024,512]{1,0:T(8,128)}, u32[]{:S(2)}) copy-start(f32[1024,512]{1,0:T(8,128)} %x_hbm.1) | copy-start | bytes 6291460
  1.6 0.7 copy-start.1

commit v4 on v3

--- a/solution.py
+++ b/solution.py
@@ -13,7 +13,7 @@
 CHUNKS = 4
 RAW = ((0, 256), (256, 192))
 PIECES = ((448, 128), (576, 192), (768, 256))
-EARLY = 2
+EARLY = 3
 RELAY = ((0, 256), (256, 192))
 MESH = pl.DeviceIdType.MESH
 

time: 69.7 us -> 71.9 us (1.032); the launches traced: 69.6 us -> 71 us
  Pallas kernels: 66 us -> 67.4 us
    pallas_call x1, Pallas kernels: 66 us -> 67.4 us  [shards(): pl.pallas_call(functools.partial(kernel, n_wide, n_rows, n_rounds), out_s...]
where the time goes in v4:
time: 71.9 us; the launch traced here: 71 us
  Pallas kernels  67.4 us (94%)
  local copies, waits for them, and re-layouts  3.6 us (5%)
    pallas_call x1, Pallas kernels, shards(): pl.pallas_call(functools.partial(kernel, n_wide, n_rows, n_rounds), out_s...  67.4 us
    unnamed x5, local copies, waits for them, and re-layouts  3.6 us

profile of v4, /device:TPU:1, one launch (start us, length us, event | category | flops | bytes accessed | tf_op | source)
XLA Modules:
  0.0 71.0 jit_solution(2048209502638940537)
XLA Ops:
  0.0 0.0 copy-start
  0.0 1.6 %copy-done = f32[1024,512]{1,0:T(8,128)S(1)} copy-done((f32[1024,512]{1,0:T(8,128)S(1)}, f32[1024,512]{1,0:T(8,128)}, u32[]{:S(2)}) %copy-start) | copy-done | bytes 2097176
  1.6 0.0 copy-start.1
  1.6 0.7 copy-done.1
  2.3 67.4 %shard_map.28 = f32[1024,512]{1,0:T(8,128)S(1)} custom-call(f32[1024,512]{1,0:T(8,128)S(1)} %copy-done, s32[2,512]{1,0:T(2,128)S(1)} %copy-done.1), custom_call_target="tpu_custom_call" | custom-call | tf_op jit(solution)/shard_map/pallas_call | solution.py:395
  69.7 1.3 %copy.4 = f32[1024,512]{1,0:T(8,128)} copy(f32[1024,512]{1,0:T(8,128)S(1)} %shard_map.28) | data formatting | bytes 4194304
Async XLA Ops:
  0.0 1.6 %copy-start = (f32[1024,512]{1,0:T(8,128)S(1)}, f32[1024,512]{1,0:T(8,128)}, u32[]{:S(2)}) copy-start(f32[1024,512]{1,0:T(8,128)} %x_hbm.1) | copy-start | bytes 6291460
  1.6 0.7 copy-start.1

commit v5 on v4

--- a/solution.py
+++ b/solution.py
@@ -13,7 +13,7 @@
 CHUNKS = 4
 RAW = ((0, 256), (256, 192))
 PIECES = ((448, 128), (576, 192), (768, 256))
-EARLY = 3
+EARLY = 1
 RELAY = ((0, 256), (256, 192))
 MESH = pl.DeviceIdType.MESH
 

time: 71.9 us -> 69.7 us (0.969); the launches traced: 71 us -> 69.6 us
  Pallas kernels: 67.4 us -> 66 us
    pallas_call x1, Pallas kernels: 67.4 us -> 66 us  [shards(): pl.pallas_call(functools.partial(kernel, n_wide, n_rows, n_rounds), out_s...]
where the time goes in v5:
time: 69.7 us; the launch traced here: 69.6 us
  Pallas kernels  66 us (95%)
  local copies, waits for them, and re-layouts  3.6 us (5%)
    pallas_call x1, Pallas kernels, shards(): pl.pallas_call(functools.partial(kernel, n_wide, n_rows, n_rounds), out_s...  66 us
    unnamed x5, local copies, waits for them, and re-layouts  3.6 us

profile of v5, /device:TPU:1, one launch (start us, length us, event | category | flops | bytes accessed | tf_op | source)
XLA Modules:
  0.0 69.6 jit_solution(12769786964667087407)
XLA Ops:
  0.0 0.0 copy-start
  0.0 1.6 %copy-done = f32[1024,512]{1,0:T(8,128)S(1)} copy-done((f32[1024,512]{1,0:T(8,128)S(1)}, f32[1024,512]{1,0:T(8,128)}, u32[]{:S(2)}) %copy-start) | copy-done | bytes 2097176
  1.6 0.0 copy-start.1
  1.6 0.7 copy-done.1
  2.3 66.0 %shard_map.28 = f32[1024,512]{1,0:T(8,128)S(1)} custom-call(f32[1024,512]{1,0:T(8,128)S(1)} %copy-done, s32[2,512]{1,0:T(2,128)S(1)} %copy-done.1), custom_call_target="tpu_custom_call" | custom-call | tf_op jit(solution)/shard_map/pallas_call | solution.py:395
  68.3 1.3 %copy.4 = f32[1024,512]{1,0:T(8,128)} copy(f32[1024,512]{1,0:T(8,128)S(1)} %shard_map.28) | data formatting | bytes 4194304
Async XLA Ops:
  0.0 1.6 %copy-start = (f32[1024,512]{1,0:T(8,128)S(1)}, f32[1024,512]{1,0:T(8,128)}, u32[]{:S(2)}) copy-start(f32[1024,512]{1,0:T(8,128)} %x_hbm.1) | copy-start | bytes 6291460
  1.6 0.7 copy-start.1
